TPU v7x, 512 devices: a whole 4x8x8 slice. The times are simulated.
512 devices in a mesh: sub: 64 (over y, z), crow: 4 (over x_lo, core), ccol: 2 (over x_hi).
Axes of the slice: x: 4 (x_hi: 2, x_lo: 2; x = x_hi * 2 + x_lo), y: 8, z: 8, core: 2. Of those that a mesh axis runs over, the one named last changes fastest.
Arguments:
- loads: bfloat16 [128, 1024, 128], P('sub'), may hold values from -6 to 6
- stiffness: bfloat16 [128, 1024, 1024], P('sub', ('crow', 'ccol'))
- local_inverse: bfloat16 [128, 1024, 1024], P('sub', ('crow', 'ccol'))
- coarse_basis: bfloat16 [128, 1024, 48], P('sub', ('crow', 'ccol')), may hold values from -0.1875 to 0.1875
- coarse_inverse: bfloat16 [6144, 6144], P('sub', ('crow', 'ccol'))
- coarse_index: int32 [128, 48], P('sub'), may hold values from 0 to 6143, as said below
- left_rows: int32 [128, 128], P('sub'), may hold values from 0 to 1023, as said below
- right_rows: int32 [128, 128], P('sub'), may hold values from 0 to 1023, as said below
Outputs:
- second_pass: float32 [128, 1024, 128], P('sub', ('crow', 'ccol'))
- final_residual: float32 [128, 1024, 128], P('sub', ('crow', 'ccol'))
Inputs may be any that keep to these rules, and one draw needn't show every extreme that they name: `coarse_index`: every value 0 to 6143 appears exactly once in the whole array. Of the 96 values in the rows of one index of sub, at most 24 lie in one block of 768 consecutive coarse rows starting at a multiple of 768, and that most is reached. In each subdomain the 128 entries of left_rows and the 128 entries of right_rows are 256 distinct rows. `right_rows`: see left_rows.
All inputs are finite; a program needn't handle non-finite values.
Results may differ from a plain program's by a relative error of at most 0.0067.
Values may be sent and summed in bfloat16 or wider, within the bound.
A program may use at most 64 MiB of HBM per device.

v0:
```python
import jax
import jax.numpy as jnp
from jax import lax
from jax.sharding import PartitionSpec as P


def padded(block, sides, width):
    for axis, dim in sides:
        count = lax.axis_size(axis)
        forward = [(i, i + 1) for i in range(count - 1)]
        forward.append((count - 1, 0))
        backward = [(target, source) for source, target in forward]
        low = lax.ppermute(
            lax.slice_in_dim(block, block.shape[dim] - width, None, axis=dim), axis, forward
        )
        high = lax.ppermute(lax.slice_in_dim(block, 0, width, axis=dim), axis, backward)
        block = jnp.concatenate([low, block, high], axis=dim)
    return block


def fold_product(matrix, gathered_piece):
    return jnp.einsum("sij,sjc->sic", matrix, gathered_piece, preferred_element_type=jnp.float32)


def apply_stiffness(iterate, stiffness, pick_left, pick_right):
    sub_count, row_count, case_count = iterate.shape
    rounded = iterate.astype(jnp.bfloat16)
    product = fold_product(stiffness, lax.all_gather(rounded, ("crow", "ccol"), axis=1, tiled=True))
    product_b = product.astype(jnp.bfloat16)
    left_part = jnp.einsum("sfi,sic->sfc", pick_left, product_b, preferred_element_type=jnp.float32)
    right_part = jnp.einsum(
        "sfi,sic->sfc", pick_right, product_b, preferred_element_type=jnp.float32
    )
    partial_faces = jnp.stack([left_part, right_part], axis=1)
    boundary = lax.psum(partial_faces.astype(jnp.bfloat16), ("crow", "ccol"))
    extended = padded(boundary, (("sub", 0),), 1)
    from_before = extended[:sub_count, 1]
    from_after = extended[2:, 0]
    added_left = jnp.einsum(
        "sfi,sfc->sic", pick_left, from_before, preferred_element_type=jnp.float32
    )
    added_right = jnp.einsum(
        "sfi,sfc->sic", pick_right, from_after, preferred_element_type=jnp.float32
    )
    return product_b.astype(jnp.float32) + added_left + added_right


def coarse_step(restricted, coarse_inverse, coarse_index):
    sub_count, mode_count, case_count = restricted.shape
    flat_rows = restricted.reshape(sub_count * mode_count, case_count)
    flat_index = coarse_index.reshape(-1)
    owned_rows, block_width = coarse_inverse.shape
    block_index = lax.axis_index(("crow", "ccol"))
    arrived, arrived_index = (
        lax.all_gather(flat_rows, "sub", axis=0, tiled=True),
        lax.all_gather(flat_index, "sub", axis=0, tiled=True),
    )
    shifted_place = arrived_index - block_index * block_width
    inside = (shifted_place >= 0) & (shifted_place < block_width)
    arrived_place = jnp.where(inside, shifted_place, block_width)
    ordered = (
        jnp.zeros((block_width + 1, case_count), jnp.bfloat16)
        .at[arrived_place]
        .set(arrived)[:block_width]
    )
    partial_coarse = jnp.dot(coarse_inverse, ordered, preferred_element_type=jnp.float32)
    coarse = lax.psum(partial_coarse, ("crow", "ccol")).astype(jnp.bfloat16)
    everything = lax.all_gather(coarse, "sub", axis=0, tiled=True)
    picked = everything[flat_index]
    return picked.reshape(sub_count, mode_count, case_count)


def precondition(local_part, residual_rows, coarse_basis, coarse_inverse, coarse_index):
    partial_modes = jnp.einsum(
        "sik,sic->skc", coarse_basis, residual_rows, preferred_element_type=jnp.float32
    )
    restricted = lax.psum(partial_modes, ("crow", "ccol")).astype(jnp.bfloat16)
    picked = coarse_step(restricted, coarse_inverse, coarse_index)
    return local_part + jnp.einsum(
        "sik,skc->sic", coarse_basis, picked, preferred_element_type=jnp.float32
    )


def body(
    loads,
    stiffness,
    local_inverse,
    coarse_basis,
    coarse_inverse,
    coarse_index,
    left_rows,
    right_rows,
):
    sub_count, row_count, iface_count = stiffness.shape
    group_index = lax.axis_index(("crow", "ccol"))
    first_row = group_index * row_count
    loads_rows = lax.dynamic_slice_in_dim(loads, first_row, row_count, 1)
    local_rows = first_row + jnp.arange(row_count, dtype=jnp.int32)
    pick_left = (left_rows[:, :, None] == local_rows[None, None, :]).astype(jnp.bfloat16)
    pick_right = (right_rows[:, :, None] == local_rows[None, None, :]).astype(jnp.bfloat16)
    first_local = jnp.einsum(
        "sij,sjc->sic", local_inverse, loads, preferred_element_type=jnp.float32
    )
    first_pass = precondition(first_local, loads_rows, coarse_basis, coarse_inverse, coarse_index)
    image_first = apply_stiffness(first_pass, stiffness, pick_left, pick_right)
    residual_b = (loads_rows.astype(jnp.float32) - image_first).astype(jnp.bfloat16)
    second_local = fold_product(
        local_inverse, lax.all_gather(residual_b, ("crow", "ccol"), axis=1, tiled=True)
    )
    second_pass = first_pass + precondition(
        second_local, residual_b, coarse_basis, coarse_inverse, coarse_index
    )
    image_second = apply_stiffness(second_pass, stiffness, pick_left, pick_right)
    final_residual = loads_rows.astype(jnp.float32) - image_second
    return (second_pass, final_residual)


def solution(mesh):
    return jax.shard_map(
        body,
        mesh=mesh,
        in_specs=(
            P("sub", None, None),
            P("sub", ("crow", "ccol"), None),
            P("sub", ("crow", "ccol"), None),
            P("sub", ("crow", "ccol"), None),
            P("sub", ("crow", "ccol")),
            P("sub", None),
            P("sub", None),
            P("sub", None),
        ),
        out_specs=(P("sub", ("crow", "ccol"), None), P("sub", ("crow", "ccol"), None)),
        check_vma=False,
    )
```

profile of v0, /device:TPU:6, one launch (start us, length us, event | category | flops | bytes accessed | tf_op | source)
XLA Modules:
  0.0 929.7 jit_solution(8455041256860478172)
XLA Ops:
  7.2 0.0 all-gather.5.cloned.1.call-start
  7.2 1.1 convolution_bitcast_fusion.4
  8.3 34.2 %psum.42 = bf16[2,48,128]{2,1,0:T(8,128)(2,1)} all-reduce(f32[2,48,128]{2,1,0:T(8,128)S(1)} %convolution_bitcast_fusion.4), channel_id=1, replica_groups=mesh['sub'=64,'crow'=4,'ccol'=2] {'crow','ccol'}, use_global_device_ids=true, to_apply=%region_0.0 | all-reduce | flops 12288 | bytes 73728 | tf_op jit(solution)/shard_map/psum | solution.py:77
  42.5 0.0 all-gather.5.cloned.1.call-update
  42.5 0.0 all-gather.7.cloned.1.call-start
  42.6 0.8 reshape.96
  43.3 1.3 dynamic-slice
  45.3 0.3 dynamic-update-slice
  45.6 282.8 %all-reduce = s32[6144]{0:T(1024)S(1)} all-reduce(s32[6144]{0:T(1024)S(1)} %dynamic-update-slice), channel_id=1, replica_groups=mesh['sub'=64,'crow'=4,'ccol'=2] {'sub'}, use_global_device_ids=true, to_apply=%add | all-reduce | flops 6144 | bytes 49152
  328.4 0.0 all-gather.5.cloned.1.call-done
  328.4 16.2 %scatter_custom_fusion = bf16[769,128]{1,0:T(8,128)(2,1)S(1)} fusion(s32[6144]{0:T(1024)S(1)} %compare_select_fusion, bf16[6144,128]{1,0:T(8,128)(2,1)} %all-gather.5.cloned.1.call-done, bf16[]{:T(256)} %constant.10.clone.1), kind=kCustom, calls=%fused_computation.46 | custom fusion | bytes 197376 | tf_op jit(solution)/shard_map/scatter | solution.py:64
  344.6 1.1 convolution_bitcast_fusion.3
  345.7 30.7 %psum.43 = bf16[96,128]{1,0:T(8,128)(2,1)} all-reduce(f32[96,128]{1,0:T(8,128)S(1)} %convolution_bitcast_fusion.3), channel_id=1, replica_groups=mesh['sub'=64,'crow'=4,'ccol'=2] {'crow','ccol'}, use_global_device_ids=true, to_apply=%region_2.3 | all-reduce | flops 12288 | bytes 73728 | tf_op jit(solution)/shard_map/psum | solution.py:67
  376.4 0.0 all-gather.7.cloned.1.call-update
  376.4 0.0 all-reduce.4.cloned.1.call-start
  376.4 0.8 reshape.58
  377.2 75.1 %all-gather.7.cloned.1.call-done = bf16[6144,128]{1,0:T(8,128)(2,1)} async-done(((bf16[96,128]{1,0:T(8,128)(2,1)}), bf16[6144,128]{1,0:T(8,128)(2,1)}) %all-gather.7.cloned.1.call-update) | async-done | bytes 1572880 | tf_op jit(solution)/shard_map/all_gather | solution.py:68
  452.4 2.2 gather_fusion
  454.6 0.9 convolution_bitcast_fusion
  455.6 0.3 fusion.64
  455.9 27.2 %all_gather.28 = bf16[2,1024,128]{2,1,0:T(8,128)(2,1)S(1)} all-gather(bf16[2,128,128]{2,1,0:T(8,128)(2,1)S(1)} %get-tuple-element.6), channel_id=1, replica_groups=mesh['sub'=64,'crow'=4,'ccol'=2] {'crow','ccol'}, dimensions={1}, use_global_device_ids=true | all-gather | bytes 589824 | tf_op jit(solution)/shard_map/all_gather | solution.py:28
  483.1 0.3 convolution_convert_fusion.1
  483.4 0.3 fusion.8
  483.7 0.3 fusion.7
  484.0 0.7 pad_maximum_fusion
  484.6 0.0 all-reduce.4.cloned.1.call-update
  484.7 0.0 all-gather.9.cloned.1.call-start
  484.7 65.4 %all-reduce.4.cloned.1.call-done = bf16[2,2,128,128]{3,2,0,1:T(8,128)(2,1)} async-done(((bf16[2,2,128,128]{3,2,0,1:T(8,128)(2,1)}), bf16[2,2,128,128]{3,2,0,1:T(8,128)(2,1)}) %all-reduce.4.cloned.1.call-update) | async-done | bytes 131088 | tf_op jit(solution)/shard_map/psum | solution.py:35
  550.1 0.9 fusion.63
  550.9 8.1 collective-permute-start.1
  559.1 1.9 collective-permute-start
  561.0 0.2 collective-permute-done.1
  561.2 1.0 fusion.14
  562.2 6.5 collective-permute-done
  568.6 1.0 fusion.6
  569.6 0.1 convolution_bitcast_fusion.2
  569.8 30.8 %psum.45 = bf16[2,48,128]{2,1,0:T(8,128)(2,1)} all-reduce(f32[2,48,128]{2,1,0:T(8,128)S(1)} %convolution_bitcast_fusion.2), channel_id=1, replica_groups=mesh['sub'=64,'crow'=4,'ccol'=2] {'crow','ccol'}, use_global_device_ids=true, to_apply=%region_4.5 | all-reduce | flops 12288 | bytes 73728 | tf_op jit(solution)/shard_map/psum | solution.py:77
  600.6 0.0 all-gather.9.cloned.1.call-update
  600.6 0.0 all-gather.11.cloned.1.call-start
  600.7 77.5 %all-gather.9.cloned.1.call-done = bf16[6144,128]{1,0:T(8,128)(2,1)} async-done(((bf16[96,128]{1,0:T(8,128)(2,1)}), bf16[6144,128]{1,0:T(8,128)(2,1)}) %all-gather.9.cloned.1.call-update) | async-done | bytes 1572880 | tf_op jit(solution)/shard_map/all_gather | solution.py:55
  678.2 16.2 %scatter_custom_fusion.1 = bf16[769,128]{1,0:T(8,128)(2,1)S(1)} fusion(s32[6144]{0:T(1024)S(1)} %compare_select_fusion, bf16[6144,128]{1,0:T(8,128)(2,1)} %all-gather.9.cloned.1.call-done, bf16[]{:T(256)} %constant.10.clone.1), kind=kCustom, calls=%fused_computation.44 | custom fusion | bytes 197376 | tf_op jit(solution)/shard_map/scatter | solution.py:64
  694.4 0.2 convolution_bitcast_fusion.1
  694.6 30.9 %psum.46 = bf16[96,128]{1,0:T(8,128)(2,1)} all-reduce(f32[96,128]{1,0:T(8,128)S(1)} %convolution_bitcast_fusion.1), channel_id=1, replica_groups=mesh['sub'=64,'crow'=4,'ccol'=2] {'crow','ccol'}, use_global_device_ids=true, to_apply=%region_6.7 | all-reduce | flops 12288 | bytes 73728 | tf_op jit(solution)/shard_map/psum | solution.py:67
  725.5 0.0 all-gather.11.cloned.1.call-update
  725.5 0.0 all-reduce.6.cloned.1.call-start
  725.6 27.3 %all_gather.29 = bf16[2,1024,128]{2,1,0:T(8,128)(2,1)S(1)} all-gather(bf16[2,128,128]{2,1,0:T(8,128)(2,1)S(1)} %fusion.6), channel_id=1, replica_groups=mesh['sub'=64,'crow'=4,'ccol'=2] {'crow','ccol'}, dimensions={1}, use_global_device_ids=true | all-gather | bytes 589824 | tf_op jit(solution)/shard_map/all_gather | solution.py:108
  752.8 52.2 %all-gather.11.cloned.1.call-done = bf16[6144,128]{1,0:T(8,128)(2,1)} async-done(((bf16[96,128]{1,0:T(8,128)(2,1)}), bf16[6144,128]{1,0:T(8,128)(2,1)}) %all-gather.11.cloned.1.call-update) | async-done | bytes 1572880 | tf_op jit(solution)/shard_map/all_gather | solution.py:68
  805.1 2.2 gather_fusion.1
  807.3 0.2 fusion.66
  807.5 1.0 fusion.65
  808.5 27.2 %all_gather.32 = bf16[2,1024,128]{2,1,0:T(8,128)(2,1)S(1)} all-gather(bf16[2,128,128]{2,1,0:T(8,128)(2,1)S(1)} %get-tuple-element.8), channel_id=1, replica_groups=mesh['sub'=64,'crow'=4,'ccol'=2] {'crow','ccol'}, dimensions={1}, use_global_device_ids=true | all-gather | bytes 589824 | tf_op jit(solution)/shard_map/all_gather | solution.py:28
  835.7 0.3 convolution_convert_fusion
  836.0 0.3 fusion.10
  836.2 0.3 fusion.9
  836.5 0.7 pad_maximum_fusion.1
  837.2 0.0 all-reduce.6.cloned.1.call-update
  837.2 65.4 %all-reduce.6.cloned.1.call-done = bf16[2,2,128,128]{3,2,0,1:T(8,128)(2,1)} async-done(((bf16[2,2,128,128]{3,2,0,1:T(8,128)(2,1)}), bf16[2,2,128,128]{3,2,0,1:T(8,128)(2,1)}) %all-reduce.6.cloned.1.call-update) | async-done | bytes 131088 | tf_op jit(solution)/shard_map/psum | solution.py:35
  902.6 0.9 fusion.62
  903.5 8.1 collective-permute-start.3
  911.6 1.9 collective-permute-start.2
  913.6 0.2 collective-permute-done.3
  913.8 1.0 fusion.11
  914.7 6.5 collective-permute-done.2
  921.2 1.6 fusion.3
  (19 shorter events, 0.1 us)
Async XLA Ops:
  7.2 448.4 %copy-start = (bf16[2,128,1024]{2,1,0:T(8,128)(2,1)S(1)}, bf16[2,128,1024]{2,1,0:T(8,128)(2,1)}, u32[]{:S(2)}) copy-start(bf16[2,128,1024]{2,1,0:T(8,128)(2,1)} %param.10) | copy-start | bytes 1572868
  7.2 448.4 %copy-start.2 = (bf16[2,1024,128]{2,1,0:T(8,128)(2,1)S(1)}, bf16[2,1024,128]{2,1,0:T(8,128)(2,1)}, u32[]{:S(2)}) copy-start(bf16[2,1024,128]{2,1,0:T(8,128)(2,1)} %param.8) | copy-start | bytes 1572868
  7.2 321.2 %all-gather.5.cloned.1.call-start = ((), (), s32[]{:S(2)}) async-start(), calls=%async_computation | async-start | bytes 1597440 | tf_op jit(solution)/shard_map/all_gather | solution.py:55
  42.5 409.8 %all-gather.7.cloned.1.call-start = ((), (), s32[]{:S(2)}) async-start(), calls=%async_computation.1 | async-start | bytes 1597440 | tf_op jit(solution)/shard_map/all_gather | solution.py:68
  328.3 154.7 %copy-start.1 = (bf16[2,128,1024]{2,1,0:T(8,128)(2,1)S(1)}, bf16[2,128,1024]{2,1,0:T(8,128)(2,1)}, u32[]{:S(2)}) copy-start(bf16[2,128,1024]{2,1,0:T(8,128)(2,1)} %param.9) | copy-start | bytes 1572868
  376.4 173.7 %all-reduce.4.cloned.1.call-start = ((), (), s32[]{:S(2)}) async-start(), calls=%async_computation.2 | async-start | bytes 262144 | tf_op jit(solution)/shard_map/psum | solution.py:35
  455.6 27.8 %copy-start.5 = (s32[2,128]{1,0:T(2,128)S(1)}, s32[2,128]{1,0:T(2,128)}, u32[]{:S(2)}) copy-start(s32[2,128]{1,0:T(2,128)} %param.15) | copy-start | bytes 3076
  455.6 28.1 %copy-start.6 = (s32[2,128]{1,0:T(2,128)S(1)}, s32[2,128]{1,0:T(2,128)}, u32[]{:S(2)}) copy-start(s32[2,128]{1,0:T(2,128)} %param.14) | copy-start | bytes 3076
  483.1 86.6 %copy-start.4 = (bf16[2,128,48]{1,2,0:T(8,128)(2,1)S(1)}, bf16[2,128,48]{1,2,0:T(8,128)(2,1)}, u32[]{:S(2)}) copy-start(bf16[2,128,48]{1,2,0:T(8,128)(2,1)} %param.11) | copy-start | bytes 73732
  483.1 211.3 %copy-start.3 = (bf16[96,768]{1,0:T(8,128)(2,1)S(1)}, bf16[96,768]{1,0:T(8,128)(2,1)}, u32[]{:S(2)}) copy-start(bf16[96,768]{1,0:T(8,128)(2,1)} %param.12) | copy-start | bytes 442372
  484.7 193.5 %all-gather.9.cloned.1.call-start = ((), (), s32[]{:S(2)}) async-start(), calls=%async_computation.3 | async-start | bytes 1597440 | tf_op jit(solution)/shard_map/all_gather | solution.py:55
  550.9 10.3 %collective-permute-start.1 = (bf16[1,2,128,128]{3,2,0,1:T(8,128)(2,1)S(1)}, bf16[1,2,128,128]{3,2,0,1:T(8,128)(2,1)S(1)}, u32[]{:S(2)}, u32[]{:S(2)}) collective-permute-start(bf16[1,2,128,128]{3,2,0,1:T(8,128)(2,1)S(1)} %get-tuple-element.5), channel_id=1, source_target_pairs={{8,0},{16,8},{24,16},{32,24},{40,32},{48,40},{56,48},{64,56},{72,6... | collective-permute-start | bytes 196616 | tf_op jit(solution)/shard_map/ppermute | solution.py:16
  559.1 9.6 %collective-permute-start = (bf16[1,2,128,128]{3,2,0,1:T(8,128)(2,1)S(1)}, bf16[1,2,128,128]{3,2,0,1:T(8,128)(2,1)S(1)}, u32[]{:S(2)}, u32[]{:S(2)}) collective-permute-start(bf16[1,2,128,128]{3,2,0,1:T(8,128)(2,1)S(1)} %get-tuple-element.4), channel_id=1, source_target_pairs={{0,8},{8,16},{16,24},{24,32},{32,40},{40,48},{48,56},{56,64},{64,7... | collective-permute-start | bytes 196616 | tf_op jit(solution)/shard_map/ppermute | solution.py:13
  600.6 204.4 %all-gather.11.cloned.1.call-start = ((), (), s32[]{:S(2)}) async-start(), calls=%async_computation.4 | async-start | bytes 1597440 | tf_op jit(solution)/shard_map/all_gather | solution.py:68
  725.5 177.1 %all-reduce.6.cloned.1.call-start = ((), (), s32[]{:S(2)}) async-start(), calls=%async_computation.5 | async-start | bytes 262144 | tf_op jit(solution)/shard_map/psum | solution.py:35
  903.5 10.3 %collective-permute-start.3 = (bf16[1,2,128,128]{3,2,0,1:T(8,128)(2,1)S(1)}, bf16[1,2,128,128]{3,2,0,1:T(8,128)(2,1)S(1)}, u32[]{:S(2)}, u32[]{:S(2)}) collective-permute-start(bf16[1,2,128,128]{3,2,0,1:T(8,128)(2,1)S(1)} %get-tuple-element.3), channel_id=1, source_target_pairs={{8,0},{16,8},{24,16},{32,24},{40,32},{48,40},{56,48},{64,56},{72,6... | collective-permute-start | bytes 196616 | tf_op jit(solution)/shard_map/ppermute | solution.py:16
  911.6 9.6 %collective-permute-start.2 = (bf16[1,2,128,128]{3,2,0,1:T(8,128)(2,1)S(1)}, bf16[1,2,128,128]{3,2,0,1:T(8,128)(2,1)S(1)}, u32[]{:S(2)}, u32[]{:S(2)}) collective-permute-start(bf16[1,2,128,128]{3,2,0,1:T(8,128)(2,1)S(1)} %get-tuple-element.2), channel_id=1, source_target_pairs={{0,8},{8,16},{16,24},{24,32},{32,40},{40,48},{48,56},{56,64},{64,7... | collective-permute-start | bytes 196616 | tf_op jit(solution)/shard_map/ppermute | solution.py:13
Sparse Core Ops, SparseCore 0:
  42.7 83.8 all-gather.4
  376.5 75.8 all-gather.6
  484.8 65.2 all-reduce.3
  600.8 77.3 all-gather.8
  725.6 79.3 all-gather.10
  837.3 65.2 all-reduce.5
where the time goes:
time: 931 us; the launch traced here: 930 us
  blocking collectives  491 us (53%)
  waiting for transfers between devices  349 us (37%)
  local copies, waits for them, and re-layouts  41.7 us (4%)
  starting transfers between devices  20.3 us (2%)
  between operations  15 us (2%)
  matrix products  11.1 us (1%)
    unnamed x1, blocking collectives  283 us
    psum x2, waiting for transfers between devices, apply_stiffness(): boundary = lax.psum(partial_faces.astype(jnp.bfloat16), ('crow', 'ccol'))  131 us
    all_gather x2, waiting for transfers between devices, coarse_step(): everything = lax.all_gather(coarse, 'sub', axis=0, tiled=True)  127 us
    all_gather x2, waiting for transfers between devices, coarse_step(): lax.all_gather(flat_rows, 'sub', axis=0, tiled=True)  77.5 us
    psum x2, blocking collectives, precondition(): restricted = lax.psum(partial_modes, ('crow', 'ccol')).astype(jnp.bfloat16)  65 us
    psum x2, blocking collectives, coarse_step(): coarse = lax.psum(partial_coarse, ('crow', 'ccol')).astype(jnp.bfloat16)  61.6 us
    all_gather x2, blocking collectives, apply_stiffness(): lax.all_gather(rounded, ('crow', 'ccol'), axis=1, tiled=True)  54.3 us
    scatter x2, local copies, waits for them, and re-layouts, coarse_step(): ordered = jnp.zeros((block_width + 1, case_count), jnp.bfloat16).at[arriv...  32.4 us
  transfers between devices with their start and end apart: 10, of which 9 were waited for; matrix products, arithmetic and copies ran while one was open for 1% of the time, Pallas kernels for 0%

commit v1 on v0

--- a/solution.py
+++ b/solution.py
@@ -2,6 +2,12 @@
 import jax.numpy as jnp
 from jax import lax
 from jax.sharding import PartitionSpec as P
+
+
+def tiled_gather(x, axis, dim):
+    size = lax.axis_size(axis)
+    repeats = [size if d == dim else 1 for d in range(x.ndim)]
+    return lax.all_to_all(jnp.tile(x, repeats), axis, split_axis=dim, concat_axis=dim, tiled=True)
 
 
 def padded(block, sides, width):
@@ -52,7 +58,7 @@
     owned_rows, block_width = coarse_inverse.shape
     block_index = lax.axis_index(("crow", "ccol"))
     arrived, arrived_index = (
-        lax.all_gather(flat_rows, "sub", axis=0, tiled=True),
+        tiled_gather(flat_rows, "sub", 0),
         lax.all_gather(flat_index, "sub", axis=0, tiled=True),
     )
     shifted_place = arrived_index - block_index * block_width

time: 931 us -> 938 us (level)
  waiting for transfers between devices: 349 us -> 280 us
  blocking collectives: 491 us -> 555 us
  starting transfers between devices: 20.3 us -> 33.7 us
    all_gather x2 -> x0, waiting for transfers between devices: 77.5 us -> none  [coarse_step(): lax.all_gather(flat_rows, 'sub', axis=0, tiled=True)]
    all_to_all x0 -> x1, blocking collectives: none -> 47.2 us  [tiled_gather(): lax.all_to_all(jnp.tile(x, repeats), axis, split_axis=dim, concat_axis=di...]
    unnamed x1, blocking collectives: 283 us -> 301 us
    all_to_all x0 -> x1, starting transfers between devices: none -> 13.4 us  [tiled_gather(): lax.all_to_all(jnp.tile(x, repeats), axis, split_axis=dim, concat_axis=di...]
  transfers between devices with their start and end apart: 10 -> 9, of which waited for: 9 -> 8; matrix products, arithmetic and copies ran while one was open for 1% -> 0% of each run, Pallas kernels for 0% -> 0%
where the time goes in v1:
time: 938 us; the launch traced here: 937 us
  blocking collectives  555 us (59%)
  waiting for transfers between devices  280 us (30%)
  local copies, waits for them, and re-layouts  42.1 us (4%)
  starting transfers between devices  33.7 us (4%)
  between operations  14.7 us (2%)
  matrix products  10.1 us (1%)
    unnamed x1, blocking collectives  301 us
    all_gather x2, waiting for transfers between devices, coarse_step(): everything = lax.all_gather(coarse, 'sub', axis=0, tiled=True)  136 us
    psum x2, waiting for transfers between devices, apply_stiffness(): boundary = lax.psum(partial_faces.astype(jnp.bfloat16), ('crow', 'ccol'))  131 us
    psum x2, blocking collectives, precondition(): restricted = lax.psum(partial_modes, ('crow', 'ccol')).astype(jnp.bfloat16)  63.9 us
    psum x2, blocking collectives, coarse_step(): coarse = lax.psum(partial_coarse, ('crow', 'ccol')).astype(jnp.bfloat16)  61.2 us
    all_gather x2, blocking collectives, apply_stiffness(): lax.all_gather(rounded, ('crow', 'ccol'), axis=1, tiled=True)  54.3 us
    all_to_all x1, blocking collectives, tiled_gather(): lax.all_to_all(jnp.tile(x, repeats), axis, split_axis=dim, concat_axis=di...  47.2 us
    scatter x2, local copies, waits for them, and re-layouts, coarse_step(): ordered = jnp.zeros((block_width + 1, case_count), jnp.bfloat16).at[arriv...  31.8 us
  transfers between devices with their start and end apart: 9, of which 8 were waited for; matrix products, arithmetic and copies ran while one was open for 0% of the time, Pallas kernels for 0%

profile of v1, /device:TPU:6, one launch (start us, length us, event | category | flops | bytes accessed | tf_op | source)
XLA Modules:
  0.0 936.9 jit_solution(3190025851106216787)
XLA Ops:
  7.2 0.0 copy-start
  7.2 1.0 convolution_bitcast_fusion.4
  8.2 33.6 %psum.42 = bf16[2,48,128]{2,1,0:T(8,128)(2,1)S(1)} all-reduce(f32[2,48,128]{2,1,0:T(8,128)S(1)} %convolution_bitcast_fusion.4), channel_id=1, replica_groups=mesh['sub'=64,'crow'=4,'ccol'=2] {'crow','ccol'}, use_global_device_ids=true, to_apply=%region_0.0 | all-reduce | flops 12288 | bytes 73728 | tf_op jit(solution)/shard_map/psum | solution.py:83
  41.9 1.4 tile.17
  43.2 13.4 %all-to-all-start = ((bf16[64,96,128]{2,1,0:T(8,128)(2,1)}), bf16[64,96,128]{2,1,0:T(8,128)(2,1)S(1)}, u32[]{:S(2)}, u32[]{:S(2)}) async-start(bf16[64,96,128]{2,1,0:T(8,128)(2,1)} %tile.17), calls=%async_computation | async-start | bytes 3145728 | tf_op jit(solution)/shard_map/all_to_all | solution.py:10
  56.6 0.0 all-gather.3.cloned.1.call-start
  56.7 0.1 reshape.102
  56.8 1.3 dynamic-slice
  58.7 0.3 dynamic-update-slice
  59.0 300.7 %all-reduce = s32[6144]{0:T(1024)S(1)} all-reduce(s32[6144]{0:T(1024)S(1)} %dynamic-update-slice), channel_id=1, replica_groups=mesh['sub'=64,'crow'=4,'ccol'=2] {'sub'}, use_global_device_ids=true, to_apply=%add | all-reduce | flops 6144 | bytes 49152
  359.7 15.9 %scatter_custom_fusion = bf16[769,128]{1,0:T(8,128)(2,1)S(1)} fusion(s32[6144]{0:T(1024)S(1)} %compare_select_fusion, bf16[6144,128]{1,0:T(8,128)(2,1)S(1)} %bitcast.68, bf16[]{:T(256)} %constant.10.clone.1), kind=kCustom, calls=%fused_computation.46 | custom fusion | bytes 196866 | tf_op jit(solution)/shard_map/scatter | solution.py:70
  375.6 0.2 convolution_bitcast_fusion.3
  375.8 31.7 %psum.43 = bf16[96,128]{1,0:T(8,128)(2,1)} all-reduce(f32[96,128]{1,0:T(8,128)S(1)} %convolution_bitcast_fusion.3), channel_id=1, replica_groups=mesh['sub'=64,'crow'=4,'ccol'=2] {'crow','ccol'}, use_global_device_ids=true, to_apply=%region_2.3 | all-reduce | flops 12288 | bytes 73728 | tf_op jit(solution)/shard_map/psum | solution.py:73
  407.5 0.0 all-gather.3.cloned.1.call-update
  407.5 0.0 all-reduce.4.cloned.1.call-start
  407.5 0.1 reshape.65
  407.6 78.8 %all-gather.3.cloned.1.call-done = bf16[6144,128]{1,0:T(8,128)(2,1)} async-done(((bf16[96,128]{1,0:T(8,128)(2,1)}), bf16[6144,128]{1,0:T(8,128)(2,1)}) %all-gather.3.cloned.1.call-update) | async-done | bytes 1572880 | tf_op jit(solution)/shard_map/all_gather | solution.py:74
  486.5 2.2 gather_fusion
  488.7 0.2 convolution_bitcast_fusion
  489.0 0.9 fusion.64
  489.9 27.2 %all_gather.21 = bf16[2,1024,128]{2,1,0:T(8,128)(2,1)S(1)} all-gather(bf16[2,128,128]{2,1,0:T(8,128)(2,1)S(1)} %get-tuple-element.6), channel_id=1, replica_groups=mesh['sub'=64,'crow'=4,'ccol'=2] {'crow','ccol'}, dimensions={1}, use_global_device_ids=true | all-gather | bytes 589824 | tf_op jit(solution)/shard_map/all_gather | solution.py:34
  517.1 0.3 convolution_convert_fusion.1
  517.4 0.3 fusion.8
  517.7 0.3 fusion.7
  518.0 0.7 pad_maximum_fusion
  518.6 0.0 all-reduce.4.cloned.1.call-update
  518.7 0.0 all-gather.5.cloned.1.call-start
  518.7 65.4 %all-reduce.4.cloned.1.call-done = bf16[2,2,128,128]{3,2,0,1:T(8,128)(2,1)} async-done(((bf16[2,2,128,128]{3,2,0,1:T(8,128)(2,1)}), bf16[2,2,128,128]{3,2,0,1:T(8,128)(2,1)}) %all-reduce.4.cloned.1.call-update) | async-done | bytes 131088 | tf_op jit(solution)/shard_map/psum | solution.py:41
  584.1 0.9 fusion.63
  585.0 8.1 collective-permute-start.1
  593.1 1.9 collective-permute-start
  595.0 0.2 collective-permute-done.1
  595.2 1.0 fusion.14
  596.2 6.5 collective-permute-done
  602.7 1.0 fusion.6
  603.7 0.6 copy-done.4
  604.3 0.1 convolution_bitcast_fusion.2
  604.4 30.3 %psum.45 = bf16[2,48,128]{2,1,0:T(8,128)(2,1)S(1)} all-reduce(f32[2,48,128]{2,1,0:T(8,128)S(1)} %convolution_bitcast_fusion.2), channel_id=1, replica_groups=mesh['sub'=64,'crow'=4,'ccol'=2] {'crow','ccol'}, use_global_device_ids=true, to_apply=%region_4.5 | all-reduce | flops 12288 | bytes 73728 | tf_op jit(solution)/shard_map/psum | solution.py:83
  634.7 0.2 tile.19
  634.9 47.2 %all_to_all.18 = bf16[64,96,128]{2,1,0:T(8,128)(2,1)S(1)} all-to-all(bf16[64,96,128]{2,1,0:T(8,128)(2,1)S(1)} %tile.19), channel_id=1, replica_groups=mesh['sub'=64,'crow'=4,'ccol'=2] {'sub'}, dimensions={0} | all-to-all | bytes 3145728 | tf_op jit(solution)/shard_map/all_to_all | solution.py:10
  682.1 15.9 %scatter_custom_fusion.1 = bf16[769,128]{1,0:T(8,128)(2,1)S(1)} fusion(s32[6144]{0:T(1024)S(1)} %compare_select_fusion, bf16[6144,128]{1,0:T(8,128)(2,1)S(1)} %bitcast.69, bf16[]{:T(256)} %constant.10.clone.1), kind=kCustom, calls=%fused_computation.44 | custom fusion | bytes 196866 | tf_op jit(solution)/shard_map/scatter | solution.py:70
  698.0 0.2 convolution_bitcast_fusion.1
  698.2 29.6 %psum.46 = bf16[96,128]{1,0:T(8,128)(2,1)} all-reduce(f32[96,128]{1,0:T(8,128)S(1)} %convolution_bitcast_fusion.1), channel_id=1, replica_groups=mesh['sub'=64,'crow'=4,'ccol'=2] {'crow','ccol'}, use_global_device_ids=true, to_apply=%region_6.7 | all-reduce | flops 12288 | bytes 73728 | tf_op jit(solution)/shard_map/psum | solution.py:73
  727.8 0.0 all-gather.5.cloned.1.call-update
  727.8 0.0 all-reduce.6.cloned.1.call-start
  727.8 27.4 %all_gather.22 = bf16[2,1024,128]{2,1,0:T(8,128)(2,1)S(1)} all-gather(bf16[2,128,128]{2,1,0:T(8,128)(2,1)} %copy-done.4), channel_id=1, replica_groups=mesh['sub'=64,'crow'=4,'ccol'=2] {'crow','ccol'}, dimensions={1}, use_global_device_ids=true | all-gather | bytes 589824 | tf_op jit(solution)/shard_map/all_gather | solution.py:114
  755.3 57.2 %all-gather.5.cloned.1.call-done = bf16[6144,128]{1,0:T(8,128)(2,1)} async-done(((bf16[96,128]{1,0:T(8,128)(2,1)}), bf16[6144,128]{1,0:T(8,128)(2,1)}) %all-gather.5.cloned.1.call-update) | async-done | bytes 1572880 | tf_op jit(solution)/shard_map/all_gather | solution.py:74
  812.4 2.4 gather_fusion.1
  814.8 0.2 fusion.66
  815.0 1.0 fusion.65
  816.0 27.2 %all_gather.24 = bf16[2,1024,128]{2,1,0:T(8,128)(2,1)S(1)} all-gather(bf16[2,128,128]{2,1,0:T(8,128)(2,1)S(1)} %get-tuple-element.8), channel_id=1, replica_groups=mesh['sub'=64,'crow'=4,'ccol'=2] {'crow','ccol'}, dimensions={1}, use_global_device_ids=true | all-gather | bytes 589824 | tf_op jit(solution)/shard_map/all_gather | solution.py:34
  843.2 0.3 convolution_convert_fusion
  843.5 0.3 fusion.10
  843.7 0.3 fusion.9
  844.0 0.7 pad_maximum_fusion.1
  844.7 0.0 all-reduce.6.cloned.1.call-update
  844.7 65.4 %all-reduce.6.cloned.1.call-done = bf16[2,2,128,128]{3,2,0,1:T(8,128)(2,1)} async-done(((bf16[2,2,128,128]{3,2,0,1:T(8,128)(2,1)}), bf16[2,2,128,128]{3,2,0,1:T(8,128)(2,1)}) %all-reduce.6.cloned.1.call-update) | async-done | bytes 131088 | tf_op jit(solution)/shard_map/psum | solution.py:41
  910.1 0.9 fusion.62
  911.0 8.1 collective-permute-start.3
  919.2 1.9 collective-permute-start.2
  921.1 0.2 collective-permute-done.3
  921.3 1.0 fusion.11
  922.2 6.5 collective-permute-done.2
  928.7 1.6 fusion.3
  (26 shorter events, 0.1 us)
Async XLA Ops:
  7.2 481.8 %copy-start = (bf16[2,128,1024]{2,1,0:T(8,128)(2,1)S(1)}, bf16[2,128,1024]{2,1,0:T(8,128)(2,1)}, u32[]{:S(2)}) copy-start(bf16[2,128,1024]{2,1,0:T(8,128)(2,1)} %param.10) | copy-start | bytes 1572868
  43.2 13.5 %copy-start.10 = (s32[2,48]{1,0:T(2,128)S(1)}, s32[2,48]{1,0:T(2,128)}, u32[]{:S(2)}) copy-start(s32[2,48]{1,0:T(2,128)} %param.13) | copy-start | bytes 1156
  43.2 332.4 %copy-start.3 = (bf16[96,768]{1,0:T(8,128)(2,1)S(1)}, bf16[96,768]{1,0:T(8,128)(2,1)}, u32[]{:S(2)}) copy-start(bf16[96,768]{1,0:T(8,128)(2,1)} %param.12) | copy-start | bytes 442372
  43.2 445.5 %copy-start.6 = (bf16[2,128,48]{1,2,0:T(8,128)(2,1)S(1)}, bf16[2,128,48]{1,2,0:T(8,128)(2,1)}, u32[]{:S(2)}) copy-start(bf16[2,128,48]{1,2,0:T(8,128)(2,1)} %param.11) | copy-start | bytes 73732
  43.2 445.7 %copy-start.2 = (bf16[2,1024,128]{2,1,0:T(8,128)(2,1)S(1)}, bf16[2,1024,128]{2,1,0:T(8,128)(2,1)}, u32[]{:S(2)}) copy-start(bf16[2,1024,128]{2,1,0:T(8,128)(2,1)} %param.8) | copy-start | bytes 1572868
  43.2 316.5 %all-to-all-start = ((bf16[64,96,128]{2,1,0:T(8,128)(2,1)}), bf16[64,96,128]{2,1,0:T(8,128)(2,1)S(1)}, u32[]{:S(2)}, u32[]{:S(2)}) async-start(bf16[64,96,128]{2,1,0:T(8,128)(2,1)} %tile.17), calls=%async_computation | async-start | bytes 3145728 | tf_op jit(solution)/shard_map/all_to_all | solution.py:10
  56.6 429.8 %all-gather.3.cloned.1.call-start = ((), (), s32[]{:S(2)}) async-start(), calls=%async_computation.2 | async-start | bytes 1597440 | tf_op jit(solution)/shard_map/all_gather | solution.py:74
  359.7 157.4 %copy-start.1 = (bf16[2,128,1024]{2,1,0:T(8,128)(2,1)S(1)}, bf16[2,128,1024]{2,1,0:T(8,128)(2,1)}, u32[]{:S(2)}) copy-start(bf16[2,128,1024]{2,1,0:T(8,128)(2,1)} %param.9) | copy-start | bytes 1572868
  407.5 176.6 %all-reduce.4.cloned.1.call-start = ((), (), s32[]{:S(2)}) async-start(), calls=%async_computation.3 | async-start | bytes 262144 | tf_op jit(solution)/shard_map/psum | solution.py:41
  407.6 82.3 %copy-start.9 = (s32[1024]{0:T(1024)}, s32[1024]{0:T(1024)S(1)}, u32[]{:S(2)}) copy-start(s32[1024]{0:T(1024)S(1)} %pad_clamp_fusion) | copy-start | bytes 12292
  488.9 28.4 %copy-start.7 = (s32[2,128]{1,0:T(2,128)S(1)}, s32[2,128]{1,0:T(2,128)}, u32[]{:S(2)}) copy-start(s32[2,128]{1,0:T(2,128)} %param.15) | copy-start | bytes 3076
  488.9 28.7 %copy-start.8 = (s32[2,128]{1,0:T(2,128)S(1)}, s32[2,128]{1,0:T(2,128)}, u32[]{:S(2)}) copy-start(s32[2,128]{1,0:T(2,128)} %param.14) | copy-start | bytes 3076
  518.7 293.8 %all-gather.5.cloned.1.call-start = ((), (), s32[]{:S(2)}) async-start(), calls=%async_computation.4 | async-start | bytes 1597440 | tf_op jit(solution)/shard_map/all_gather | solution.py:74
  585.0 10.3 %collective-permute-start.1 = (bf16[1,2,128,128]{3,2,0,1:T(8,128)(2,1)S(1)}, bf16[1,2,128,128]{3,2,0,1:T(8,128)(2,1)S(1)}, u32[]{:S(2)}, u32[]{:S(2)}) collective-permute-start(bf16[1,2,128,128]{3,2,0,1:T(8,128)(2,1)S(1)} %get-tuple-element.5), channel_id=1, source_target_pairs={{8,0},{16,8},{24,16},{32,24},{40,32},{48,40},{56,48},{64,56},{72,6... | collective-permute-start | bytes 196616 | tf_op jit(solution)/shard_map/ppermute | solution.py:22
  593.1 9.6 %collective-permute-start = (bf16[1,2,128,128]{3,2,0,1:T(8,128)(2,1)S(1)}, bf16[1,2,128,128]{3,2,0,1:T(8,128)(2,1)S(1)}, u32[]{:S(2)}, u32[]{:S(2)}) collective-permute-start(bf16[1,2,128,128]{3,2,0,1:T(8,128)(2,1)S(1)} %get-tuple-element.4), channel_id=1, source_target_pairs={{0,8},{8,16},{16,24},{24,32},{32,40},{40,48},{48,56},{56,64},{64,7... | collective-permute-start | bytes 196616 | tf_op jit(solution)/shard_map/ppermute | solution.py:19
  603.6 0.6 copy-start.4
  698.0 117.0 %copy-start.5 = (f32[2,128,128]{2,1,0:T(8,128)S(1)}, f32[2,128,128]{2,1,0:T(8,128)}, u32[]{:S(2)}) copy-start(f32[2,128,128]{2,1,0:T(8,128)} %get-tuple-element.7) | copy-start | bytes 393220
  727.8 182.3 %all-reduce.6.cloned.1.call-start = ((), (), s32[]{:S(2)}) async-start(), calls=%async_computation.5 | async-start | bytes 262144 | tf_op jit(solution)/shard_map/psum | solution.py:41
  911.0 10.3 %collective-permute-start.3 = (bf16[1,2,128,128]{3,2,0,1:T(8,128)(2,1)S(1)}, bf16[1,2,128,128]{3,2,0,1:T(8,128)(2,1)S(1)}, u32[]{:S(2)}, u32[]{:S(2)}) collective-permute-start(bf16[1,2,128,128]{3,2,0,1:T(8,128)(2,1)S(1)} %get-tuple-element.3), channel_id=1, source_target_pairs={{8,0},{16,8},{24,16},{32,24},{40,32},{48,40},{56,48},{64,56},{72,6... | collective-permute-start | bytes 196616 | tf_op jit(solution)/shard_map/ppermute | solution.py:22
  919.2 9.6 %collective-permute-start.2 = (bf16[1,2,128,128]{3,2,0,1:T(8,128)(2,1)S(1)}, bf16[1,2,128,128]{3,2,0,1:T(8,128)(2,1)S(1)}, u32[]{:S(2)}, u32[]{:S(2)}) collective-permute-start(bf16[1,2,128,128]{3,2,0,1:T(8,128)(2,1)S(1)} %get-tuple-element.2), channel_id=1, source_target_pairs={{0,8},{8,16},{16,24},{24,32},{32,40},{40,48},{48,56},{56,64},{64,7... | collective-permute-start | bytes 196616 | tf_op jit(solution)/shard_map/ppermute | solution.py:19
Sparse Core Ops, SparseCore 0:
  407.6 78.8 all-gather.2
  518.8 65.2 all-reduce.3
  727.9 84.4 all-gather.4
  844.8 65.2 all-reduce.5
